TPU v7x, 32 devices: a whole 2x2x4 slice. The times are simulated.
32 devices in a mesh: grp: 2 (over x), region: 8 (over z, y), donor: 2 (over core).
Axes of the slice: x: 2, y: 2, z: 4, core: 2. Of those that a mesh axis runs over, the one named last changes fastest.
Arguments:
- dosage: bfloat16 [16384, 8192], P(('grp', 'region'), 'donor'), parts along dimension 0, may hold values from 0 to 2, as said below
- expression: bfloat16 [512, 8192], P(('grp', 'region'), 'donor'), parts along dimension 0, may hold values from -60 to 60
- cis_tiles: int32 [512, 8], P(('grp', 'region')), parts along dimension 0, may hold values from 0 to 63, as said below
Outputs:
- correlation: float32 [512, 1024], P(('grp', 'region'), 'donor'), parts along dimension 0
- pvalue: float32 [512, 1024], P(('grp', 'region'), 'donor'), parts along dimension 0
There are 2 independent parts, one for each index of `grp`. A program takes and returns all parts, laid end to end along the dimension named above; each array names one. Nothing has to cross between parts.
Inputs may be any that keep to these rules, and one draw needn't show every extreme that they name: `dosage`: imputed dosages, within the bounds. `cis_tiles`: each gene's 8 cis tiles are consecutive tile numbers; for the genes of region block r (rows r * 32 to (r + 1) * 32 - 1) they lie from r * 8 - 8 to (r + 1) * 8 + 7, and both ends are reached in every block where they exist.
All inputs are finite; a program needn't handle non-finite values.
Results may differ from a plain program's by a relative error of at most 0.0044.
Values may be sent and summed in bfloat16 or wider, within the bound.
A program may use at most 128 MiB of HBM per device.

v0:
```python
import math
import jax
import jax.numpy as jnp
from jax import lax
from jax.sharding import PartitionSpec as P

TILE = 128
RIM = 8
CF_TERMS = 32


def with_halo(array, sides, width):
    for axis, dim in sides:
        count, length = (lax.axis_size(axis), array.shape[dim])
        up = [(i, (i + 1) % count) for i in range(count - 1)]
        down = [(j, i) for i, j in up]
        last = lax.slice_in_dim(array, length - width, length, axis=dim)
        leading = lax.slice_in_dim(array, 0, width, axis=dim)
        before = lax.ppermute(last, axis, up)
        after = lax.ppermute(leading, axis, down)
        array = jnp.concatenate([before, array, after], axis=dim)
    return array


def beta_log_constant(shape_a):
    inverse = 1.0 / shape_a
    ratio = (
        0.5 * math.log(shape_a)
        - inverse / 8.0
        + inverse**3 / 192.0
        + inverse**5 / 640.0
        - 17.0 * inverse**7 / 14336.0
    )
    return ratio - 0.5 * math.log(math.pi)


def scale_rows(values, totals, squares, count):
    center = totals / count
    spread = squares / count - center * center
    return (
        (values.astype(jnp.float32) - center[:, None]) * lax.rsqrt(spread + 1e-05)[:, None]
    ).astype(jnp.bfloat16)


def donor_product(left_rows, right_rows):
    return lax.dot_general(
        left_rows, right_rows, (((1,), (1,)), ((), ())), preferred_element_type=jnp.float32
    )


def tail_probability(squared, shape_a, log_const, terms):
    narrow = squared < 1.5 / (shape_a + 2.5)
    first = jnp.where(narrow, 0.5, shape_a)
    second = jnp.where(narrow, shape_a, 0.5)
    argument = jnp.where(narrow, squared, 1.0 - squared)
    total_ab = first + second

    def odd_term(index):
        return (
            -(first + index)
            * (total_ab + index)
            * argument
            / ((first + 2.0 * index) * (first + 2.0 * index + 1.0))
        )

    def even_term(index):
        return (
            index
            * (second - index)
            * argument
            / ((first + 2.0 * index - 1.0) * (first + 2.0 * index))
        )

    def advance(carried, coefficient):
        upper_ratio, lower_ratio, estimate = carried
        lower_ratio = 1.0 / (1.0 + coefficient * lower_ratio)
        upper_ratio = 1.0 + coefficient / upper_ratio
        return (upper_ratio, lower_ratio, estimate * lower_ratio * upper_ratio)

    def sweep(turn, carried):
        for offset in range(4):
            index = (4 * turn + offset + 1).astype(jnp.float32)
            carried = advance(carried, even_term(index))
            carried = advance(carried, odd_term(index))
        return carried

    leading = 1.0 / (1.0 - total_ab * argument / (first + 1.0))
    start = (jnp.ones_like(squared), leading, leading)
    carried = lax.fori_loop(0, terms // 4, sweep, start)
    estimate = carried[2]
    front = jnp.sqrt(squared) * jnp.exp(shape_a * jnp.log1p(-squared) + log_const)
    share = front * estimate / first
    return jnp.where(narrow, 1.0 - share, share)


def shards(dosage, expression, cis_tiles):
    donor_total = dosage.shape[1] * lax.axis_size("donor")
    gene_count = expression.shape[0]
    block_tiles = dosage.shape[0] // TILE
    rim_rows = RIM * TILE
    dose_total = jnp.sum(dosage, axis=1, dtype=jnp.float32)
    dose_square = jnp.sum(jnp.square(dosage.astype(jnp.float32)), axis=1)
    expr_total = jnp.sum(expression, axis=1, dtype=jnp.float32)
    expr_square = jnp.sum(jnp.square(expression.astype(jnp.float32)), axis=1)
    moments = lax.psum((dose_total, dose_square, expr_total, expr_square), "donor")
    zdose = scale_rows(dosage, moments[0], moments[1], donor_total)
    zexpr = scale_rows(expression, moments[2], moments[3], donor_total)
    widened = with_halo(zdose, (("region", 0),), rim_rows)
    dense = donor_product(zexpr, widened)
    first_tile = lax.axis_index("region") * block_tiles - RIM
    local_tile = cis_tiles - first_tile
    layered = dense.reshape(gene_count, block_tiles + 2 * RIM, TILE)
    index_grid = jnp.broadcast_to(local_tile[:, :, None], (gene_count, local_tile.shape[1], TILE))
    picked = jnp.take_along_axis(layered, index_grid, axis=1)
    partial_pairs = picked.reshape(gene_count, local_tile.shape[1] * TILE)
    share_width = partial_pairs.shape[1] // lax.axis_size("donor")
    summed = lax.psum(partial_pairs, "donor")
    own_pairs = lax.dynamic_slice_in_dim(
        summed, lax.axis_index("donor") * share_width, share_width, 1
    )
    correlation = own_pairs / donor_total
    squared = jnp.minimum(correlation * correlation, 0.9)
    shape_a = (donor_total - 2) / 2.0
    log_const = beta_log_constant(shape_a)
    pvalue = tail_probability(squared, shape_a, log_const, CF_TERMS)
    return (correlation, pvalue)


def solution(mesh):
    in_specs = (
        P(("grp", "region"), "donor"),
        P(("grp", "region"), "donor"),
        P(("grp", "region"), None),
    )
    out_specs = (P(("grp", "region"), "donor"), P(("grp", "region"), "donor"))
    return jax.shard_map(shards, mesh=mesh, in_specs=in_specs, out_specs=out_specs, check_vma=False)
```

profile of v0, /device:TPU:0, one launch (start us, length us, event | category | flops | bytes accessed | tf_op | source)
XLA Modules:
  0.0 695.8 jit_solution(16506730900923522625)
XLA Ops:
  7.2 0.0 copy-start.1
  7.2 0.0 all-reduce.3.cloned.1.call-start
  7.2 6.0 convert_reduce_fusion
  13.2 0.0 copy-done.1
  13.2 0.2 convert_reduce_fusion.1
  13.4 2.6 all-reduce
  16.0 0.0 copy-start.2
  16.1 11.0 %fusion.9 = bf16[1024,4096]{1,0:T(8,128)(2,1)} fusion(bf16[1024,4096]{1,0:T(8,128)(2,1)} %param.5, f32[1024]{0:T(1024)S(1)} %get-tuple-element.298, f32[1024]{0:T(1024)S(1)} %get-tuple-element.297), kind=kLoop, calls=%fused_computation.46 | loop fusion | flops 16777216 | bytes 16785408 | tf_op jit(solution)/shard_map/convert_element_type | solution.py:42
  27.1 8.0 %collective-permute-start = (bf16[1024,4096]{1,0:T(8,128)(2,1)}, bf16[1024,4096]{1,0:T(8,128)(2,1)}, u32[]{:S(2)}, u32[]{:S(2)}) collective-permute-start(bf16[1024,4096]{1,0:T(8,128)(2,1)} %fusion.9), channel_id=1, source_target_pairs={{0,2},{2,4},{4,6},{6,8},{8,10},{10,12},{12,14},{1,3},{3,5},{5,7},{... | collective-permute-start | bytes 25165832 | tf_op jit(solution)/shard_map/ppermute | solution.py:19
  35.0 1.3 collective-permute-start.1
  36.3 0.0 copy-done.2
  36.4 0.1 copy.13
  36.4 0.1 copy.12
  36.5 0.1 copy.11
  36.6 0.2 or_bitcast_fusion
  36.8 355.1 %collective-permute-done = bf16[1024,4096]{1,0:T(8,128)(2,1)} collective-permute-done((bf16[1024,4096]{1,0:T(8,128)(2,1)}, bf16[1024,4096]{1,0:T(8,128)(2,1)}, u32[]{:S(2)}, u32[]{:S(2)}) %collective-permute-start) | collective-permute-done | bytes 8388640 | tf_op jit(solution)/shard_map/ppermute | solution.py:19
  391.9 0.0 collective-permute-done.1
  391.9 11.8 %fusion.11 = f32[4,8,24,128]{3,1,2,0:T(8,128)S(1)} fusion(bf16[1024,4096]{1,0:T(8,128)(2,1)} %collective-permute-done.1, bf16[1024,4096]{1,0:T(8,128)(2,1)} %fusion.9, bf16[1024,4096]{1,0:T(8,128)(2,1)} %collective-permute-done, bf16[32,4096]{1,0:T(8,128)(2,1)S(1)} %copy-done.1, f32[32]{0:T(128)S(1)} %get-tuple-element.300, f32[32]{0:T(128)S(1)} %get-tuple-element.299), kind=kOutput, calls=%fused_computation.48 | convolution fusion | flops 881328128 | bytes 25821440 | tf_op jit(solution)/shard_map/dot_general | solution.py:46
  403.8 0.1 copy.17
  403.8 259.4 %gather_fusion = f32[32768]{0:T(1024)S(1)} fusion(f32[32,24,128]{2,1,0:T(8,128)S(1)} %bitcast.11, s32[32768]{0:T(1024)S(1)} %or_bitcast_fusion), kind=kCustom, calls=%fused_computation | custom fusion | bytes 655360 | tf_op jit(solution)/shard_map/jit(take_along_axis)/gather | solution.py:114
  663.2 0.2 bitcast_select_fusion
  663.4 0.7 copy.20
  664.1 0.0 all-reduce.3.cloned.1.call-update
  664.1 20.2 %all-reduce.3.cloned.1.call-done = f32[32,1024]{1,0:T(8,128)} async-done(((f32[32,1024]{1,0:T(8,128)}), f32[32,1024]{1,0:T(8,128)}) %all-reduce.3.cloned.1.call-update) | async-done | bytes 131088 | tf_op jit(solution)/shard_map/psum | solution.py:117
  684.3 0.9 broadcast_select_fusion
  685.2 0.0 copy-start
  685.3 3.0 while.21
  685.3 0.3 multiply_multiply_fusion.10
  685.7 0.3 multiply_multiply_fusion.10
  686.0 0.3 multiply_multiply_fusion.10
  686.4 0.3 multiply_multiply_fusion.10
  686.8 0.3 multiply_multiply_fusion.10
  687.2 0.3 multiply_multiply_fusion.10
  687.5 0.3 multiply_multiply_fusion.10
  687.9 0.3 multiply_multiply_fusion.10
  688.2 0.7 subtract_select_fusion
  689.0 0.0 copy-done
  (7 shorter events, 0.1 us)
Async XLA Ops:
  7.2 6.0 copy-start.1
  7.2 677.1 %all-reduce.3.cloned.1.call-start = ((), (), s32[]{:S(2)}) async-start(), calls=%async_computation | async-start | bytes 262144 | tf_op jit(solution)/shard_map/psum | solution.py:117
  16.0 20.3 %copy-start.2 = (s32[32,8]{0,1:T(8,128)S(1)}, s32[32,8]{0,1:T(8,128)}, u32[]{:S(2)}) copy-start(s32[32,8]{0,1:T(8,128)} %param.7) | copy-start | bytes 3076
  27.1 364.8 %collective-permute-start = (bf16[1024,4096]{1,0:T(8,128)(2,1)}, bf16[1024,4096]{1,0:T(8,128)(2,1)}, u32[]{:S(2)}, u32[]{:S(2)}) collective-permute-start(bf16[1024,4096]{1,0:T(8,128)(2,1)} %fusion.9), channel_id=1, source_target_pairs={{0,2},{2,4},{4,6},{6,8},{8,10},{10,12},{12,14},{1,3},{3,5},{5,7},{... | collective-permute-start | bytes 25165832 | tf_op jit(solution)/shard_map/ppermute | solution.py:19
  35.0 356.9 %collective-permute-start.1 = (bf16[1024,4096]{1,0:T(8,128)(2,1)}, bf16[1024,4096]{1,0:T(8,128)(2,1)}, u32[]{:S(2)}, u32[]{:S(2)}) collective-permute-start(bf16[1024,4096]{1,0:T(8,128)(2,1)} %fusion.9), channel_id=1, source_target_pairs={{2,0},{4,2},{6,4},{8,6},{10,8},{12,10},{14,12},{3,1},{5,3},{7,5},{... | collective-permute-start | bytes 25165832 | tf_op jit(solution)/shard_map/ppermute | solution.py:20
  685.2 3.8 copy-start
Sparse Core Ops, SparseCore 0:
  664.2 20.0 all-reduce.2
where the time goes:
time: 696 us
  waiting for transfers between devices  375 us (54%)
  local copies, waits for them, and re-layouts  260 us (37%)
  other arithmetic  21.9 us (3%)
  between operations  14.2 us (2%)
  matrix products  11.8 us (2%)
  starting transfers between devices  9.27 us (1%)
    ppermute x1, waiting for transfers between devices, with_halo(): before = lax.ppermute(last, axis, up)  355 us
    gather x1, local copies, waits for them, and re-layouts, shards(): picked = jnp.take_along_axis(layered, index_grid, axis=1)  259 us
    psum x1, waiting for transfers between devices, shards(): summed = lax.psum(partial_pairs, 'donor')  20.2 us
  transfers between devices with their start and end apart: 3, of which 2 were waited for; matrix products, arithmetic and copies ran while one was open for 0% of the time, Pallas kernels for 0%

commit v1 on v0

--- a/solution.py
+++ b/solution.py
@@ -114,7 +114,7 @@
     picked = jnp.take_along_axis(layered, index_grid, axis=1)
     partial_pairs = picked.reshape(gene_count, local_tile.shape[1] * TILE)
     share_width = partial_pairs.shape[1] // lax.axis_size("donor")
-    summed = lax.psum(partial_pairs, "donor")
+    summed = jnp.sum(lax.all_gather(partial_pairs, "donor"), axis=0)
     own_pairs = lax.dynamic_slice_in_dim(
         summed, lax.axis_index("donor") * share_width, share_width, 1
     )

time: 696 us -> 664 us (0.954)
  waiting for transfers between devices: 375 us -> 355 us
  between operations: 14.2 us -> 0.79 us
    psum x1 -> x0, waiting for transfers between devices: 20.2 us -> none  [shards(): summed = lax.psum(partial_pairs, 'donor')]
  transfers between devices with their start and end apart: 3 -> 2, of which waited for: 2 -> 1; matrix products, arithmetic and copies ran while one was open for 0% -> 0% of each run, Pallas kernels for 0% -> 0%
where the time goes in v1:
time: 664 us; the launch traced here: 663 us
  waiting for transfers between devices  355 us (53%)
  local copies, waits for them, and re-layouts  260 us (39%)
  other arithmetic  21.1 us (3%)
  matrix products  11.8 us (2%)
  starting transfers between devices  9.24 us (1%)
    ppermute x1, waiting for transfers between devices, with_halo(): before = lax.ppermute(last, axis, up)  355 us
    gather x1, local copies, waits for them, and re-layouts, shards(): picked = jnp.take_along_axis(layered, index_grid, axis=1)  259 us
  transfers between devices with their start and end apart: 2, of which 1 were waited for; matrix products, arithmetic and copies ran while one was open for 0% of the time, Pallas kernels for 0%

profile of v1, /device:TPU:0, one launch (start us, length us, event | category | flops | bytes accessed | tf_op | source)
XLA Modules:
  0.0 662.7 jit_solution(5264704266022263820)
XLA Ops:
  0.6 0.0 copy-start.1
  0.6 6.0 convert_reduce_fusion
  6.6 0.0 copy-done.1
  6.6 0.2 convert_reduce_fusion.1
  6.8 2.6 all-reduce
  9.5 0.0 copy-start.2
  9.5 11.0 %fusion.9 = bf16[1024,4096]{1,0:T(8,128)(2,1)} fusion(bf16[1024,4096]{1,0:T(8,128)(2,1)} %param.5, f32[1024]{0:T(1024)S(1)} %get-tuple-element.298, f32[1024]{0:T(1024)S(1)} %get-tuple-element.297), kind=kLoop, calls=%fused_computation.46 | loop fusion | flops 16777216 | bytes 16785408 | tf_op jit(solution)/shard_map/convert_element_type | solution.py:42
  20.5 8.0 %collective-permute-start = (bf16[1024,4096]{1,0:T(8,128)(2,1)}, bf16[1024,4096]{1,0:T(8,128)(2,1)}, u32[]{:S(2)}, u32[]{:S(2)}) collective-permute-start(bf16[1024,4096]{1,0:T(8,128)(2,1)} %fusion.9), channel_id=1, source_target_pairs={{0,2},{2,4},{4,6},{6,8},{8,10},{10,12},{12,14},{1,3},{3,5},{5,7},{... | collective-permute-start | bytes 25165832 | tf_op jit(solution)/shard_map/ppermute | solution.py:19
  28.5 1.3 collective-permute-start.1
  29.8 0.0 copy-done.2
  29.8 0.1 copy.19
  29.9 0.1 copy.18
  30.0 0.1 copy.17
  30.1 0.2 or_bitcast_fusion
  30.3 355.1 %collective-permute-done = bf16[1024,4096]{1,0:T(8,128)(2,1)} collective-permute-done((bf16[1024,4096]{1,0:T(8,128)(2,1)}, bf16[1024,4096]{1,0:T(8,128)(2,1)}, u32[]{:S(2)}, u32[]{:S(2)}) %collective-permute-start) | collective-permute-done | bytes 8388640 | tf_op jit(solution)/shard_map/ppermute | solution.py:19
  385.4 0.0 collective-permute-done.1
  385.4 11.8 %fusion.11 = f32[4,8,24,128]{3,1,2,0:T(8,128)S(1)} fusion(bf16[1024,4096]{1,0:T(8,128)(2,1)} %collective-permute-done.1, bf16[1024,4096]{1,0:T(8,128)(2,1)} %fusion.9, bf16[1024,4096]{1,0:T(8,128)(2,1)} %collective-permute-done, bf16[32,4096]{1,0:T(8,128)(2,1)S(1)} %copy-done.1, f32[32]{0:T(128)S(1)} %get-tuple-element.300, f32[32]{0:T(128)S(1)} %get-tuple-element.299), kind=kOutput, calls=%fused_computation.48 | convolution fusion | flops 881328128 | bytes 25821440 | tf_op jit(solution)/shard_map/dot_general | solution.py:46
  397.2 0.1 copy.23
  397.3 259.4 %gather_fusion = f32[32768]{0:T(1024)S(1)} fusion(f32[32,24,128]{2,1,0:T(8,128)S(1)} %bitcast.7, s32[32768]{0:T(1024)S(1)} %or_bitcast_fusion), kind=kCustom, calls=%fused_computation | custom fusion | bytes 655360 | tf_op jit(solution)/shard_map/jit(take_along_axis)/gather | solution.py:114
  656.7 0.2 bitcast_select_fusion
  656.9 2.0 all_gather.3
  658.9 0.0 copy-start
  659.0 3.0 while.21
  659.0 0.3 multiply_multiply_fusion.10
  659.4 0.3 multiply_multiply_fusion.10
  659.8 0.3 multiply_multiply_fusion.10
  660.1 0.3 multiply_multiply_fusion.10
  660.5 0.3 multiply_multiply_fusion.10
  660.9 0.3 multiply_multiply_fusion.10
  661.3 0.3 multiply_multiply_fusion.10
  661.6 0.3 multiply_multiply_fusion.10
  662.0 0.7 subtract_select_fusion
  662.7 0.0 copy-done
  (10 shorter events, 0.2 us)
Async XLA Ops:
  0.6 6.0 copy-start.1
  9.5 20.3 %copy-start.2 = (s32[32,8]{0,1:T(8,128)S(1)}, s32[32,8]{0,1:T(8,128)}, u32[]{:S(2)}) copy-start(s32[32,8]{0,1:T(8,128)} %param.7) | copy-start | bytes 3076
  20.5 364.8 %collective-permute-start = (bf16[1024,4096]{1,0:T(8,128)(2,1)}, bf16[1024,4096]{1,0:T(8,128)(2,1)}, u32[]{:S(2)}, u32[]{:S(2)}) collective-permute-start(bf16[1024,4096]{1,0:T(8,128)(2,1)} %fusion.9), channel_id=1, source_target_pairs={{0,2},{2,4},{4,6},{6,8},{8,10},{10,12},{12,14},{1,3},{3,5},{5,7},{... | collective-permute-start | bytes 25165832 | tf_op jit(solution)/shard_map/ppermute | solution.py:19
  28.5 356.9 %collective-permute-start.1 = (bf16[1024,4096]{1,0:T(8,128)(2,1)}, bf16[1024,4096]{1,0:T(8,128)(2,1)}, u32[]{:S(2)}, u32[]{:S(2)}) collective-permute-start(bf16[1024,4096]{1,0:T(8,128)(2,1)} %fusion.9), channel_id=1, source_target_pairs={{2,0},{4,2},{6,4},{8,6},{10,8},{12,10},{14,12},{3,1},{5,3},{7,5},{... | collective-permute-start | bytes 25165832 | tf_op jit(solution)/shard_map/ppermute | solution.py:20
  658.9 3.8 copy-start
